TPU v7x, 512 devices: a whole 4x8x8 slice. The times are simulated.
512 devices in a mesh: flop: 4 (over x), turn: 16 (over y, core), river: 8 (over z).
Axes of the slice: x: 4, y: 8, z: 8, core: 2. Of those that a mesh axis runs over, the one named last changes fastest.
Arguments:
- regrets: float32 [4, 256, 1326], P('flop', ('turn', 'river')), may hold values from -6 to 6
- opp_reach: bfloat16 [4, 256, 1326], P('flop', ('turn', 'river')), may hold values from 0 to 1
- pot_size: int32 [4, 256], P('flop', ('turn', 'river')), may hold values from 1 to 8
- line_kind: int32 [4, 256], P('flop', ('turn', 'river')), may hold values from 0 to 2
- board_lines: int32 [4, 16, 16, 256], P('flop', 'turn', 'river'), may hold values from 0 to 255, as said below
- board_count: int32 [4, 16, 16], P('flop', 'turn', 'river'), may hold values from 64 to 256, as said below
- hand_ranks: int32 [4, 16, 16, 1326], P('flop', 'turn', 'river'), may hold values from 0 to 7461
- live_hands: int32 [4, 16, 16, 1326], P('flop', 'turn', 'river'), may hold values 0 or 1
Outputs:
- new_regrets: float32 [4, 256, 1326], P('flop', ('turn', 'river'))
- chance_values: float32 [128, 1326], P(('turn', 'river'))
Inputs may be any that keep to these rules, and one draw needn't show every extreme that they name: `board_lines`: each board lists 256 different lines of its flop; its first board_count slots hold the lines live on it, the other slots add nothing. `board_count`: in every flop one board has all 256 slots live and another only 64.
All inputs are finite; a program needn't handle non-finite values. No bound on the sum of `live_hands` on one device may be relied on, other than what follows from the above.
Results may differ from a plain program's by a relative error of at most 0.0003.
Values may be sent and summed in bfloat16 or wider, within the bound.
A program may use at most 64 MiB of HBM per device.

v0:
```python
import jax
import jax.numpy as jnp
import numpy as np
from jax import lax
from jax.sharding import PartitionSpec as P

CARDS = 52
ACTS = 2
floor_share = 0.1


def disjoint_table(card_count):
    card_first, card_second = np.triu_indices(card_count, 1)
    first_cards = jnp.asarray(card_first.astype(np.int32))
    second_cards = jnp.asarray(card_second.astype(np.int32))
    apart = (first_cards[:, None] != first_cards[None, :]) & (
        first_cards[:, None] != second_cards[None, :]
    )
    apart = (
        apart
        & (second_cards[:, None] != first_cards[None, :])
        & (second_cards[:, None] != second_cards[None, :])
    )
    return apart


def payoff_matrix(board_ranks, board_live, apart):
    both_live = apart & (board_live[:, None] > 0) & (board_live[None, :] > 0)
    fold_part = both_live.astype(jnp.float32)
    ordering = jnp.sign(board_ranks[None, :] - board_ranks[:, None]).astype(jnp.float32)
    return jnp.concatenate([fold_part * ordering, fold_part], axis=1).astype(jnp.bfloat16)


def on_device(
    regrets, opp_reach, pot_size, line_kind, board_lines, board_count, hand_ranks, live_hands
):
    hand_count = opp_reach.shape[2]
    boards_here = board_lines.shape[2]
    board_total = lax.axis_size("turn") * lax.axis_size("river") * boards_here
    pot_float = pot_size.astype(jnp.float32)
    show_coef = jnp.where(line_kind == 0, pot_float, 0.0)
    fold_coef = jnp.where(line_kind == 1, -pot_float, jnp.where(line_kind == 2, pot_float, 0.0))
    line_coef = jnp.stack([show_coef, fold_coef], axis=2).astype(jnp.bfloat16)
    reach_whole, coef_whole = (
        lax.all_gather(opp_reach, ("turn", "river"), axis=1, tiled=True),
        lax.all_gather(line_coef, ("turn", "river"), axis=1, tiled=True),
    )
    reach_whole = reach_whole[0]
    coef_whole = coef_whole[0]
    line_total = reach_whole.shape[0]
    slot_total = board_lines.shape[3]
    apart = disjoint_table(CARDS)
    chance_scale = 1.0 / (board_total * hand_count)
    line_table = jnp.zeros((line_total, hand_count), jnp.float32)
    for board_index in range(boards_here):
        slot_lines = board_lines[0, 0, board_index]
        live_count = board_count[0, 0, board_index]
        slot_reach = jnp.take(reach_whole, slot_lines, axis=0)
        slot_coef = jnp.take(coef_whole, slot_lines, axis=0).astype(jnp.float32)
        matrix = payoff_matrix(hand_ranks[0, 0, board_index], live_hands[0, 0, board_index], apart)

        def evaluate(
            first_row,
            row_count,
            slot_reach=slot_reach,
            slot_coef=slot_coef,
            matrix=matrix,
            live_count=live_count,
        ):
            products = jnp.dot(slot_reach, matrix, preferred_element_type=jnp.float32)
            slot_ids = first_row + jnp.arange(row_count, dtype=jnp.int32)
            keep_mask = (slot_ids < live_count).astype(jnp.float32)
            board_value = (
                slot_coef[:, 0:1] * products[:, :hand_count]
                + slot_coef[:, 1:2] * products[:, hand_count:]
            )
            return board_value * (chance_scale * keep_mask)[:, None]

        values = evaluate(0, slot_total)
        position = (
            jnp.full((line_total,), slot_total, jnp.int32)
            .at[slot_lines]
            .set(jnp.arange(slot_total, dtype=jnp.int32))
        )
        padded_values = jnp.concatenate([values, jnp.zeros((1, hand_count), jnp.float32)], axis=0)
        line_table = line_table + jnp.take(padded_values, position, axis=0)
    line_values = lax.psum_scatter(
        lax.slice_in_dim(
            line_table, 0, regrets.shape[1] * lax.axis_size(("turn", "river")), axis=0
        ),
        ("turn", "river"),
        scatter_dimension=0,
        tiled=True,
    )
    held_regret = regrets[0]
    group_total = held_regret.shape[0] // ACTS
    grouped = held_regret.reshape(group_total, ACTS, hand_count)
    worth_lines = line_values.reshape(group_total, ACTS, hand_count)
    positive = jnp.maximum(grouped, 0.0)
    strategy = (positive + floor_share) / (
        jnp.sum(positive, axis=1, keepdims=True) + ACTS * floor_share
    )
    node_values = jnp.sum(strategy * worth_lines, axis=1)
    updated = jnp.maximum(grouped + worth_lines - node_values[:, None, :], 0.0).reshape(
        held_regret.shape
    )
    chance_values = lax.psum(node_values, "flop") / lax.axis_size("flop")
    return (updated[None], chance_values)


def solution(mesh):
    placed = (
        P("flop", ("turn", "river"), None),
        P("flop", ("turn", "river"), None),
        P("flop", ("turn", "river")),
        P("flop", ("turn", "river")),
        P("flop", "turn", "river", None),
        P("flop", "turn", "river"),
        P("flop", "turn", "river", None),
        P("flop", "turn", "river", None),
    )
    return jax.shard_map(
        on_device,
        mesh=mesh,
        in_specs=placed,
        out_specs=(P("flop", ("turn", "river"), None), P(("turn", "river"), None)),
        check_vma=False,
    )
```

profile of v0, /device:TPU:24, one launch (start us, length us, event | category | flops | bytes accessed | tf_op | source)
XLA Modules:
  0.0 440.4 jit_solution(8097442302047093316)
XLA Ops:
  7.2 0.0 copy-start.9
  7.2 0.0 copy-start.8
  7.2 0.0 all-reduce.5.cloned.1.call-start
  7.2 0.8 fusion.31
  8.0 0.8 compare_select_fusion.1
  8.8 0.7 copy.27
  9.5 94.9 %all_gather.7 = bf16[1,256,1326]{2,0,1:T(2,128)(2,1)S(1)} all-gather(bf16[1,2,1326]{2,0,1:T(2,128)(2,1)S(1)} %copy.27), channel_id=1, replica_groups=mesh['flop'=4,'turn'=16,'river'=8] {'turn','river'}, dimensions={1}, use_global_device_ids=true | all-gather | bytes 684216 | tf_op jit(solution)/shard_map/all_gather | solution.py:45
  104.4 0.1 copy.39
  104.5 0.0 copy-done.9
  104.5 0.0 copy-done.8
  104.6 0.1 copy.24
  104.7 67.3 %all_gather.6 = bf16[1,256,2]{2,0,1:T(2,128)(2,1)S(1)} all-gather(bf16[1,2,2]{2,0,1:T(2,128)(2,1)S(1)} %copy.24), channel_id=1, replica_groups=mesh['flop'=4,'turn'=16,'river'=8] {'turn','river'}, dimensions={1}, use_global_device_ids=true | all-gather | bytes 1032 | tf_op jit(solution)/shard_map/all_gather | solution.py:46
  172.0 0.1 copy.25
  172.1 0.1 copy.26
  172.2 1.3 gather_fusion.1
  173.6 0.9 gather_fusion
  174.4 0.0 copy-start.6
  174.4 0.0 copy-start.5
  174.4 0.0 copy-start.7
  174.5 0.0 copy-start.2
  174.5 0.0 copy-start.3
  174.5 2.1 gather_fusion.4
  176.6 0.9 gather_fusion.3
  177.5 1.4 scatter_custom_fusion
  178.9 1.4 scatter_custom_fusion.1
  180.3 0.0 copy-done.6
  180.3 0.1 compare_reduce_fusion.1
  180.4 0.0 copy-done.5
  180.4 0.1 select_convert_fusion.3
  180.5 0.2 slice_reduce_fusion.3
  180.7 0.0 copy-done.7
  180.8 0.6 fusion.32
  181.3 0.6 compare_select_fusion.7
  182.0 0.0 copy-done.2
  182.0 0.0 copy-done.3
  182.0 5.2 %convert_convert_fusion.1 = (bf16[1326,1326]{1,0:T(8,128)(2,1)S(1)}, bf16[1326,1326]{1,0:T(8,128)(2,1)}) fusion(pred[1326]{0:T(1024)(128)(4,1)S(1)} %get-tuple-element.11, s32[1326]{0:T(1024)S(1)} %copy-done.3, s32[1326]{0:T(1024)S(1)} %copy-done.2, pred[1326]{0:T(1024)(128)(4,1)S(1)} %get-tuple-element.12), kind=kLoop, calls=%fused_computation.10 | loop fusion | flops 26374140 | bytes 7046364 | tf_op jit(solution)/shard_map/convert.3
  187.2 8.7 %select_convert_fusion.1 = (bf16[1326,1326]{1,0:T(8,128)(2,1)S(1)}, bf16[1326,1326]{1,0:T(8,128)(2,1)}) fusion(s32[1326]{0:T(1024)S(1)} %get-tuple-element.9, pred[1326]{0:T(1024)(128)(4,1)S(1)} %get-tuple-element.11, s32[1326]{0:T(1024)S(1)} %copy-done.3, s32[1326]{0:T(1024)S(1)} %copy-done.2, s32[1326]{0:T(1024)S(1)} %get-tuple-element.10, ...), kind=kLoop, calls=%fused_computation.11 | loop fusion | flops 36923796 | bytes 7056972 | tf_op jit(solution)/shard_map/convert.2
  196.0 5.3 %fusion = f32[256,2652]{0,1:T(8,128)S(1)} fusion(bf16[1326,1326]{1,0:T(8,128)(2,1)S(1)} %get-tuple-element.15, bf16[1326,1326]{1,0:T(8,128)(2,1)S(1)} %get-tuple-element.13, bf16[256,1326]{1,0:T(8,128)(2,1)S(1)} %gather_fusion.1, pred[256]{0:T(512)(128)(4,1)S(1)} %compare_and_fusion.4), kind=kOutput, calls=%fused_computation.15 | convolution fusion | flops 1814880256 | bytes 10427920 | tf_op jit(solution)/shard_map/dot_general | solution.py:70
  201.3 0.3 fusion.11
  201.6 0.4 copy.36
  202.0 0.1 select_convert_fusion.2
  202.1 0.2 slice_reduce_fusion.1
  202.3 0.7 compare_select_fusion.6
  203.0 8.6 %fusion.4 = f32[256,2652]{0,1:T(8,128)S(1)} fusion(bf16[1326,1326]{1,0:T(8,128)(2,1)} %get-tuple-element.16, bf16[1326,1326]{1,0:T(8,128)(2,1)} %get-tuple-element.14, bf16[256,1326]{1,0:T(8,128)(2,1)} %gather_fusion.4, pred[256]{0:T(512)(128)(4,1)S(1)} %compare_and_fusion.2), kind=kOutput, calls=%fused_computation.19 | convolution fusion | flops 1814880256 | bytes 10427920 | tf_op jit(solution)/shard_map/dot_general | solution.py:70
  211.6 0.3 fusion.9
  211.8 1.6 copy.37
  213.4 0.0 copy-start.1
  213.4 0.1 concatenate.24.clone
  213.5 1.3 copy-done.1
  214.8 0.1 concatenate.26.clone
  214.9 2.3 gather_fusion.2
  217.2 0.0 copy-start
  217.2 2.3 gather_fusion.5
  219.5 0.0 copy-done
  219.5 0.0 copy-start.4
  219.5 2.7 select_add_fusion
  222.2 0.0 all-reduce.5.cloned.1.call-update
  222.2 1.3 dynamic-slice
  224.2 0.0 copy-done.4
  224.2 196.0 %all-reduce.5.cloned.1.call-done = f32[256,1326]{1,0:T(8,128)} async-done(((f32[256,1326]{1,0:T(8,128)}), f32[256,1326]{1,0:T(8,128)}) %all-reduce.5.cloned.1.call-update) | async-done | bytes 1357840
  420.2 0.8 fusion.18
  421.1 10.5 %psum.7 = f32[1,1326]{1,0:T(1,128)S(1)} all-reduce(f32[1,1326]{1,0:T(1,128)S(1)} %reduce_sum.22), channel_id=1, replica_groups=mesh['flop'=4,'turn'=16,'river'=8] {'flop'}, use_global_device_ids=true, to_apply=%region_5.9 | all-reduce | flops 1326 | bytes 10608 | tf_op jit(solution)/shard_map/psum | solution.py:107
  431.6 0.6 broadcast_multiply_fusion
  432.2 1.4 subtract_maximum_fusion
  (19 shorter events, 0.1 us)
Async XLA Ops:
  7.2 97.4 %copy-start.9 = (s32[1,2]{1,0:T(1,128)S(1)}, s32[1,2]{1,0:T(1,128)}, u32[]{:S(2)}) copy-start(s32[1,2]{1,0:T(1,128)} %param.18) | copy-start | bytes 28
  7.2 97.4 %copy-start.8 = (s32[1,2]{1,0:T(1,128)S(1)}, s32[1,2]{1,0:T(1,128)}, u32[]{:S(2)}) copy-start(s32[1,2]{1,0:T(1,128)} %param.19) | copy-start | bytes 28
  7.2 413.1 %all-reduce.5.cloned.1.call-start = ((), (), s32[]{:S(2)}) async-start(), calls=%async_computation | async-start | bytes 2883584
  174.4 5.9 %copy-start.6 = (s32[1,1,2,1326]{3,2,1,0:T(2,128)S(1)}, s32[1,1,2,1326]{3,2,1,0:T(2,128)}, u32[]{:S(2)}) copy-start(s32[1,1,2,1326]{3,2,1,0:T(2,128)} %param.23) | copy-start | bytes 31828
  174.4 6.0 %copy-start.5 = (s32[1,1,2,1326]{3,2,1,0:T(2,128)S(1)}, s32[1,1,2,1326]{3,2,1,0:T(2,128)}, u32[]{:S(2)}) copy-start(s32[1,1,2,1326]{3,2,1,0:T(2,128)} %param.22) | copy-start | bytes 31828
  174.4 6.3 %copy-start.7 = (s32[1,1,2]{2,1,0:T(1,128)S(1)}, s32[1,1,2]{2,1,0:T(1,128)}, u32[]{:S(2)}) copy-start(s32[1,1,2]{2,1,0:T(1,128)} %param.21) | copy-start | bytes 28
  174.5 7.5 %copy-start.2 = (s32[1326]{0:T(1024)S(1)}, s32[1326]{0:T(1024)}, u32[]{:S(2)}) copy-start(s32[1326]{0:T(1024)} %constant.44.clone) | copy-start | bytes 15916
  174.5 7.5 %copy-start.3 = (s32[1326]{0:T(1024)S(1)}, s32[1326]{0:T(1024)}, u32[]{:S(2)}) copy-start(s32[1326]{0:T(1024)} %constant.45.clone) | copy-start | bytes 15916
  213.4 1.4 copy-start.1
  217.2 2.3 copy-start
  219.5 4.7 %copy-start.4 = (f32[1,2,1326]{2,1,0:T(2,128)S(1)}, f32[1,2,1326]{2,1,0:T(2,128)}, u32[]{:S(2)}) copy-start(f32[1,2,1326]{2,1,0:T(2,128)} %param.16) | copy-start | bytes 31828
Sparse Core Ops, SparseCore 0:
  222.3 197.8 all-reduce.4
where the time goes:
time: 441 us; the launch traced here: 440 us
  waiting for transfers between devices  196 us (44%)
  blocking collectives  173 us (39%)
  other arithmetic  22.5 us (5%)
  local copies, waits for them, and re-layouts  20.2 us (5%)
  between operations  15 us (3%)
  matrix products  13.9 us (3%)
    unnamed x2, waiting for transfers between devices  196 us
    all_gather x1, blocking collectives, on_device(): lax.all_gather(opp_reach, ('turn', 'river'), axis=1, tiled=True)  94.9 us
    all_gather x1, blocking collectives, on_device(): lax.all_gather(line_coef, ('turn', 'river'), axis=1, tiled=True)  67.3 us
    another operation x2, other arithmetic  14 us
    dot_general x2, matrix products, evaluate(): products = jnp.dot(slot_reach, matrix, preferred_element_type=jnp.float32)  13.9 us
    psum x1, blocking collectives, on_device(): chance_values = lax.psum(node_values, 'flop') / lax.axis_size('flop')  10.5 us
  transfers between devices with their start and end apart: 1, of which 1 were waited for; matrix products, arithmetic and copies ran while one was open for 0% of the time, Pallas kernels for 0%

commit v1 on v0

--- a/solution.py
+++ b/solution.py
@@ -43,7 +43,12 @@
     line_coef = jnp.stack([show_coef, fold_coef], axis=2).astype(jnp.bfloat16)
     reach_whole, coef_whole = (
         lax.all_gather(opp_reach, ("turn", "river"), axis=1, tiled=True),
-        lax.all_gather(line_coef, ("turn", "river"), axis=1, tiled=True),
+        jnp.concatenate(
+            lax.all_to_all(
+                jnp.stack([line_coef] * lax.axis_size(("turn", "river"))), ("turn", "river"), 0, 0
+            ),
+            axis=1,
+        ),
     )
     reach_whole = reach_whole[0]
     coef_whole = coef_whole[0]

time: 441 us -> 391 us (0.89)
  blocking collectives: 173 us -> 99.1 us
  starting transfers between devices: 0.04 us -> 17.4 us
    all_gather x1 -> x0, blocking collectives: 67.3 us -> none  [on_device(): lax.all_gather(line_coef, ('turn', 'river'), axis=1, tiled=True)]
    all_to_all x0 -> x1, starting transfers between devices: none -> 17.3 us  [on_device(): lax.all_to_all(jnp.stack([line_coef] * lax.axis_size(('turn', 'river'))),...]
    all_gather x1, blocking collectives: 94.9 us -> 88.6 us  [on_device(): lax.all_gather(opp_reach, ('turn', 'river'), axis=1, tiled=True)]
  transfers between devices with their start and end apart: 1 -> 2, of which waited for: 1 -> 1; matrix products, arithmetic and copies ran while one was open for 0% -> 10% of each run, Pallas kernels for 0% -> 0%
where the time goes in v1:
time: 391 us; the launch traced here: 390 us
  waiting for transfers between devices  198 us (51%)
  blocking collectives  99.1 us (25%)
  other arithmetic  26.2 us (7%)
  local copies, waits for them, and re-layouts  20.6 us (5%)
  starting transfers between devices  17.4 us (4%)
  between operations  15 us (4%)
  matrix products  13.5 us (3%)
    unnamed x2, waiting for transfers between devices  198 us
    all_gather x1, blocking collectives, on_device(): lax.all_gather(opp_reach, ('turn', 'river'), axis=1, tiled=True)  88.6 us
    all_to_all x1, starting transfers between devices, on_device(): lax.all_to_all(jnp.stack([line_coef] * lax.axis_size(('turn', 'river'))),...  17.3 us
    dot_general x2, matrix products, evaluate(): products = jnp.dot(slot_reach, matrix, preferred_element_type=jnp.float32)  13.5 us
    another operation x2, other arithmetic  12.6 us
    psum x1, blocking collectives, on_device(): chance_values = lax.psum(node_values, 'flop') / lax.axis_size('flop')  10.5 us
  transfers between devices with their start and end apart: 2, of which 1 were waited for; matrix products, arithmetic and copies ran while one was open for 10% of the time, Pallas kernels for 0%

profile of v1, /device:TPU:24, one launch (start us, length us, event | category | flops | bytes accessed | tf_op | source)
XLA Modules:
  0.0 390.1 jit_solution(3814621316308221795)
XLA Ops:
  7.2 0.7 fusion.20
  7.9 0.1 copy.22
  8.0 0.7 stack.11
  8.6 17.3 %all-to-all-start = ((bf16[128,1,2,2]{3,2,1,0:T(2,128)(2,1)}), bf16[128,1,2,2]{3,2,1,0:T(2,128)(2,1)S(1)}, u32[]{:S(2)}, u32[]{:S(2)}) async-start(bf16[128,1,2,2]{3,2,1,0:T(2,128)(2,1)} %stack.11), calls=%async_computation | async-start | bytes 131072 | tf_op jit(solution)/shard_map/all_to_all | solution.py:47
  26.0 0.0 copy-start.5
  26.0 0.0 all-reduce.5.cloned.1.call-start
  26.0 0.8 fusion.31
  26.8 0.8 compare_select_fusion.1
  27.6 1.4 scatter_custom_fusion
  29.0 1.4 scatter_custom_fusion.1
  30.5 0.8 compare_reduce_fusion.1
  31.3 0.8 slice_reduce_fusion.5
  32.1 0.7 copy.23
  32.8 88.6 %all_gather.3 = bf16[1,256,1326]{2,0,1:T(2,128)(2,1)S(1)} all-gather(bf16[1,2,1326]{2,0,1:T(2,128)(2,1)S(1)} %copy.23), channel_id=1, replica_groups=mesh['flop'=4,'turn'=16,'river'=8] {'turn','river'}, dimensions={1}, use_global_device_ids=true | all-gather | bytes 684216 | tf_op jit(solution)/shard_map/all_gather | solution.py:45
  121.4 0.1 copy.34
  121.5 0.0 copy-done.5
  121.5 0.6 fusion.32
  122.1 0.6 compare_select_fusion.7
  122.8 1.3 gather_fusion.1
  124.1 0.0 copy-start.2
  124.1 0.0 copy-start.3
  124.1 1.3 gather_fusion.4
  125.4 0.0 copy-done.2
  125.4 0.0 copy-done.3
  125.5 4.4 %convert_convert_fusion.1 = (bf16[1326,1326]{1,0:T(8,128)(2,1)S(1)}, bf16[1326,1326]{1,0:T(8,128)(2,1)S(1)}) fusion(pred[1326]{0:T(1024)(128)(4,1)S(1)} %get-tuple-element.11, s32[1326]{0:T(1024)S(1)} %copy-done.3, s32[1326]{0:T(1024)S(1)} %copy-done.2, pred[1326]{0:T(1024)(128)(4,1)S(1)} %get-tuple-element.12), kind=kLoop, calls=%fused_computation.10 | loop fusion | flops 26374140 | bytes 7046364 | tf_op jit(solution)/shard_map/convert.3
  129.8 8.2 %select_convert_fusion.1 = (bf16[1326,1326]{1,0:T(8,128)(2,1)S(1)}, bf16[1326,1326]{1,0:T(8,128)(2,1)S(1)}) fusion(s32[1326]{0:T(1024)S(1)} %get-tuple-element.9, pred[1326]{0:T(1024)(128)(4,1)S(1)} %get-tuple-element.11, s32[1326]{0:T(1024)S(1)} %copy-done.3, s32[1326]{0:T(1024)S(1)} %copy-done.2, s32[1326]{0:T(1024)S(1)} %get-tuple-element.10, ...), kind=kLoop, calls=%fused_computation.11 | loop fusion | flops 36923796 | bytes 7056972 | tf_op jit(solution)/shard_map/convert.2
  138.1 6.8 %fusion = f32[256,2652]{0,1:T(8,128)} fusion(bf16[1326,1326]{1,0:T(8,128)(2,1)S(1)} %get-tuple-element.15, bf16[1326,1326]{1,0:T(8,128)(2,1)S(1)} %get-tuple-element.13, bf16[256,1326]{1,0:T(8,128)(2,1)S(1)} %gather_fusion.1, pred[256]{0:T(512)(128)(4,1)S(1)} %compare_and_fusion.4), kind=kOutput, calls=%fused_computation.15 | convolution fusion | flops 1814880256 | bytes 10427920 | tf_op jit(solution)/shard_map/dot_general | solution.py:75
  144.8 6.7 %fusion.4 = f32[256,2652]{0,1:T(8,128)} fusion(bf16[1326,1326]{1,0:T(8,128)(2,1)S(1)} %get-tuple-element.16, bf16[1326,1326]{1,0:T(8,128)(2,1)S(1)} %get-tuple-element.14, bf16[256,1326]{1,0:T(8,128)(2,1)S(1)} %gather_fusion.4, pred[256]{0:T(512)(128)(4,1)S(1)} %compare_and_fusion.2), kind=kOutput, calls=%fused_computation.19 | convolution fusion | flops 1814880256 | bytes 10427920 | tf_op jit(solution)/shard_map/dot_general | solution.py:75
  151.6 0.6 compare_select_fusion.6
  152.2 0.0 all-to-all-done
  152.2 0.9 gather_fusion
  153.1 0.9 gather_fusion.3
  154.0 0.1 select_convert_fusion.3
  154.1 0.2 slice_reduce_fusion.3
  154.3 2.0 fusion.11
  156.3 0.4 copy.31
  156.7 0.1 select_convert_fusion.2
  156.8 0.2 slice_reduce_fusion.1
  157.0 2.2 fusion.9
  159.3 1.6 copy.32
  160.8 0.0 copy-start.1
  160.8 0.1 concatenate.23.clone
  160.9 1.3 copy-done.1
  162.2 0.1 concatenate.25.clone
  162.3 2.3 gather_fusion.2
  164.6 0.0 copy-start
  164.6 2.3 gather_fusion.5
  166.9 0.0 copy-done
  166.9 0.0 copy-start.4
  166.9 2.7 select_add_fusion
  169.6 0.0 all-reduce.5.cloned.1.call-update
  169.7 1.3 dynamic-slice
  171.6 0.0 copy-done.4
  171.6 198.3 %all-reduce.5.cloned.1.call-done = f32[256,1326]{1,0:T(8,128)} async-done(((f32[256,1326]{1,0:T(8,128)}), f32[256,1326]{1,0:T(8,128)}) %all-reduce.5.cloned.1.call-update) | async-done | bytes 1357840
  369.9 0.8 fusion.18
  370.7 10.5 %psum.7 = f32[1,1326]{1,0:T(1,128)S(1)} all-reduce(f32[1,1326]{1,0:T(1,128)S(1)} %reduce_sum.22), channel_id=1, replica_groups=mesh['flop'=4,'turn'=16,'river'=8] {'flop'}, use_global_device_ids=true, to_apply=%region_5.9 | all-reduce | flops 1326 | bytes 10608 | tf_op jit(solution)/shard_map/psum | solution.py:112
  381.2 0.6 broadcast_multiply_fusion
  381.8 1.4 subtract_maximum_fusion
  (17 shorter events, 0.1 us)
Async XLA Ops:
  8.6 143.6 %all-to-all-start = ((bf16[128,1,2,2]{3,2,1,0:T(2,128)(2,1)}), bf16[128,1,2,2]{3,2,1,0:T(2,128)(2,1)S(1)}, u32[]{:S(2)}, u32[]{:S(2)}) async-start(bf16[128,1,2,2]{3,2,1,0:T(2,128)(2,1)} %stack.11), calls=%async_computation | async-start | bytes 131072 | tf_op jit(solution)/shard_map/all_to_all | solution.py:47
  26.0 95.5 %copy-start.5 = (s32[1,1,2]{2,1,0:T(1,128)S(1)}, s32[1,1,2]{2,1,0:T(1,128)}, u32[]{:S(2)}) copy-start(s32[1,1,2]{2,1,0:T(1,128)} %param.21) | copy-start | bytes 28
  26.0 343.9 %all-reduce.5.cloned.1.call-start = ((), (), s32[]{:S(2)}) async-start(), calls=%async_computation.1 | async-start | bytes 2883584
  124.1 1.3 copy-start.2
  124.1 1.3 copy-start.3
  160.8 1.4 copy-start.1
  164.6 2.3 copy-start
  166.9 4.7 %copy-start.4 = (f32[1,2,1326]{2,1,0:T(2,128)S(1)}, f32[1,2,1326]{2,1,0:T(2,128)}, u32[]{:S(2)}) copy-start(f32[1,2,1326]{2,1,0:T(2,128)} %param.16) | copy-start | bytes 31828
Sparse Core Ops, SparseCore 0:
  169.8 200.0 all-reduce.4
